TPU v7x, 512 devices: a whole 4x8x8 slice. The times are simulated.
512 devices in a mesh: replica: 32 (over x, y), table: 16 (over z, core).
Axes of the slice: x: 4, y: 8, z: 8, core: 2. Of those that a mesh axis runs over, the one named last changes fastest.
Arguments:
- emb_table: float32 [16384, 128], P('table'), may hold values from -3 to 3
- row_accum: float32 [16384], P('table'), may hold values from 0.001 to 1
- look_rows: int32 [32, 16, 16, 4, 312], P('replica', 'table'), may hold values from 0 to 1023
- live_counts: int32 [32, 16, 16], P('replica'), may hold values from 1 to 312, 3328 in all within a row
- bag_order: int32 [32, 16, 3328], P('replica', 'table'), may hold values from 0 to 3327, each once within a row
- dense_emb: bfloat16 [65536, 128], P(('replica', 'table')), may hold values from -6 to 6
- labels: int32 [65536], P(('replica', 'table')), may hold values 0 or 1
- cross_in: bfloat16 [3456, 512], P('table'), may hold values from -0.109375 to 0.109375
- cross_out: bfloat16 [3456, 512], P('table'), may hold values from -0.25 to 0.25
- cross_bias: float32 [3456], replicated, may hold values from -3 to 3
- head_weight: float32 [3456], replicated, may hold values from -0.109375 to 0.109375
Outputs:
- logits: float32 [65536], P(('replica', 'table'))
- row_update: float32 [16384, 128], P('table')
- new_accum: float32 [16384], P('table')
Inputs may be any that keep to these rules, and one draw needn't show every extreme that they name: `look_rows`: local row numbers within shard s; entries in unused slots are ignored. `live_counts`: for each replica and owner the counts over shards sum to 3328; for each of them some shard sends exactly 312. `bag_order`: each of an owner's 3328 bags appears once.
All inputs are finite; a program needn't handle non-finite values. No bound on the sum of `labels` on one device may be relied on, other than what follows from the above.
Results may differ from a plain program's by a relative error of at most 0.0045.
Values may be sent and summed in bfloat16 or wider, within the bound.
A program may use at most 64 MiB of HBM per device.

v0:
```python
import jax
import jax.numpy as jnp
from jax import lax
from jax.sharding import PartitionSpec as P

EPSILON = 1e-08


def bag_sources(live_row, permute, capacity):
    bag_count = permute.shape[0]
    slot_ends = jnp.cumsum(live_row)
    counter = jnp.arange(bag_count, dtype=jnp.int32)
    passed = (counter[:, None] >= slot_ends[None, :]).astype(jnp.int32)
    source = jnp.sum(passed, axis=1)
    before = jnp.sum(passed * live_row[None, :], axis=1)
    flat_slot = source * capacity + (counter - before)
    inverse = jnp.zeros((bag_count,), jnp.int32).at[permute].set(counter)
    return flat_slot[inverse]


def slot_bags(live_row, permute, capacity):
    bag_count = permute.shape[0]
    starts = jnp.cumsum(live_row) - live_row
    column = jnp.arange(capacity, dtype=jnp.int32)
    position = jnp.minimum(starts[:, None] + column[None, :], bag_count - 1)
    is_live = column[None, :] < live_row[:, None]
    return (permute[position], is_live)


def local(
    emb_table,
    row_accum,
    look_rows,
    live_counts,
    bag_order,
    dense_emb,
    labels,
    cross_in,
    cross_out,
    cross_bias,
    head_weight,
):
    shards = lax.axis_size("table")
    own_index = lax.axis_index("table")
    feature_width = emb_table.shape[1]
    hot_count = look_rows.shape[3]
    capacity = look_rows.shape[4]
    contract = (((1,), (1,)), ((), ()))
    row_ids = look_rows[0, 0]
    pool_sum = jnp.take(emb_table, row_ids[:, 0].reshape(-1), axis=0)
    for member in range(1, hot_count):
        pool_sum = pool_sum + jnp.take(emb_table, row_ids[:, member].reshape(-1), axis=0)
    slot_pool = pool_sum.astype(jnp.bfloat16).reshape(shards, capacity, feature_width)
    arrived = lax.all_to_all(slot_pool, "table", split_axis=0, concat_axis=0, tiled=True)
    live_row = lax.dynamic_index_in_dim(live_counts[0], own_index, 0, keepdims=False)
    permute = bag_order[0, 0]
    bag_slot = bag_sources(live_row, permute, capacity)
    batch_size = dense_emb.shape[0]
    pooled = jnp.take(arrived.reshape(-1, feature_width), bag_slot, axis=0).reshape(batch_size, -1)
    cross_input = jnp.concatenate([dense_emb, pooled], axis=1)
    full_in, full_out = (
        lax.all_gather(cross_in, "table", axis=0, tiled=True),
        lax.all_gather(cross_out, "table", axis=0, tiled=True),
    )
    hidden = jnp.dot(cross_input, full_in, preferred_element_type=jnp.float32).astype(jnp.bfloat16)
    mixed_rows = (
        lax.dot_general(hidden, full_out, contract, preferred_element_type=jnp.float32) + cross_bias
    )
    crossed = cross_input * mixed_rows + cross_input
    logits = jnp.dot(crossed, head_weight, precision=lax.Precision.HIGHEST)
    logit_grad = jax.nn.sigmoid(logits) - labels.astype(jnp.float32)
    cross_grad = logit_grad[:, None] * head_weight[None, :]
    mixed_grad = (cross_grad * cross_input).astype(jnp.bfloat16)
    hidden_grad = jnp.dot(mixed_grad, full_out, preferred_element_type=jnp.float32).astype(
        jnp.bfloat16
    )
    back_term = lax.dot_general(hidden_grad, full_in, contract, preferred_element_type=jnp.float32)
    input_grad = cross_grad * (mixed_rows + 1.0) + back_term
    pooled_grad = input_grad[:, feature_width:].astype(jnp.bfloat16).reshape(-1, feature_width)
    bag_ids, is_live = slot_bags(live_row, permute, capacity)
    outgoing = jnp.take(pooled_grad, bag_ids.reshape(-1), axis=0).reshape(
        shards, capacity, feature_width
    )
    outgoing = jnp.where(is_live[:, :, None], outgoing, jnp.zeros_like(outgoing))
    returned = lax.all_to_all(outgoing, "table", split_axis=0, concat_axis=0, tiled=True)
    returned_rows = returned.astype(jnp.float32).reshape(-1, feature_width)
    local_grads = jnp.zeros(emb_table.shape, jnp.float32)
    for member in range(hot_count):
        local_grads = local_grads.at[row_ids[:, member].reshape(-1)].add(returned_rows)
    summed = lax.psum(local_grads, "replica")
    new_accum = row_accum + jnp.mean(summed * summed, axis=1)
    row_update = -summed / (jnp.sqrt(new_accum)[:, None] + EPSILON)
    return (logits, row_update, new_accum)


def solution(mesh):
    placed = (
        P("table", None),
        P("table"),
        P("replica", "table", None, None, None),
        P("replica", None, None),
        P("replica", "table", None),
        P(("replica", "table"), None),
        P(("replica", "table")),
        P("table", None),
        P("table", None),
        P(),
        P(),
    )
    return jax.shard_map(
        local,
        mesh=mesh,
        in_specs=placed,
        out_specs=(P(("replica", "table")), P("table", None), P("table")),
        check_vma=False,
    )
```

profile of v0, /device:TPU:1, one launch (start us, length us, event | category | flops | bytes accessed | tf_op | source)
XLA Modules:
  0.0 485.7 jit_solution(4508932941182334574)
XLA Ops:
  8.7 1.4 slice_reduce_fusion.3
  10.7 8.2 %gather_fusion.6 = f32[4992,128]{1,0:T(8,128)S(1)} fusion(f32[1024,128]{1,0:T(8,128)S(1)} %copy-done, s32[5120]{0:T(1024)S(1)} %pad_clamp_fusion.3), kind=kCustom, calls=%fused_computation.2.clone | custom fusion | bytes 5131776 | tf_op jit(solution)/shard_map/jit(_take)/gather | solution.py:52
  18.9 10.1 %gather_fusion.7 = f32[4992,128]{1,0:T(8,128)} fusion(f32[1024,128]{1,0:T(8,128)S(1)} %copy-done, s32[5120]{0:T(1024)S(1)} %pad_clamp_fusion.2), kind=kCustom, calls=%fused_computation.3.clone | custom fusion | bytes 5131776 | tf_op jit(solution)/shard_map/jit(_take)/gather | solution.py:52
  29.0 10.1 %gather_fusion.4 = f32[4992,128]{1,0:T(8,128)} fusion(f32[1024,128]{1,0:T(8,128)S(1)} %copy-done, s32[5120]{0:T(1024)S(1)} %pad_clamp_fusion.5), kind=kCustom, calls=%fused_computation.clone | custom fusion | bytes 5131776 | tf_op jit(solution)/shard_map/jit(_take)/gather | solution.py:50
  39.2 10.1 %gather_fusion.5 = f32[4992,128]{1,0:T(8,128)} fusion(f32[1024,128]{1,0:T(8,128)S(1)} %copy-done, s32[5120]{0:T(1024)S(1)} %pad_clamp_fusion.4), kind=kCustom, calls=%fused_computation.1.clone | custom fusion | bytes 5131776 | tf_op jit(solution)/shard_map/jit(_take)/gather | solution.py:52
  49.4 6.9 %fusion.8 = bf16[4992,128]{1,0:T(8,128)(2,1)} fusion(f32[4992,128]{1,0:T(8,128)} %gather_fusion.7, f32[4992,128]{1,0:T(8,128)S(1)} %gather_fusion.6, f32[4992,128]{1,0:T(8,128)} %gather_fusion.5, f32[4992,128]{1,0:T(8,128)} %gather_fusion.4, pred[4992]{0:T(1024)(128)(4,1)S(1)} %get-tuple-element.16, pred[4992]{0:T(1024)(128)(4,1)S(1)} %get-tuple-element.17, ...), kind=kLoop, calls=%fused_computation.24 | loop fusion | flops 5111808 | bytes 11521536 | tf_op jit(solution)/shard_map/convert_element_type | solution.py:53
  56.3 11.8 %all-to-all-start = ((bf16[16,312,128]{2,1,0:T(8,128)(2,1)}), bf16[16,312,128]{2,1,0:T(8,128)(2,1)S(1)}, u32[]{:S(2)}, u32[]{:S(2)}) async-start(bf16[16,312,128]{2,1,0:T(8,128)(2,1)} %bitcast.28), calls=%async_computation | async-start | bytes 2555904 | tf_op jit(solution)/shard_map/all_to_all | solution.py:54
  69.1 12.9 %scatter_custom_fusion = s32[3328]{0:T(1024)S(1)} fusion(s32[3328]{0:T(1024)S(1)} %fusion.22, s32[3328]{0:T(1024)S(1)} %iota.19, s32[]{:T(128)} %constant.31.clone.1), kind=kCustom, calls=%fused_computation.90 | custom fusion | bytes 13316 | tf_op jit(solution)/shard_map/scatter | solution.py:17
  82.1 0.7 fusion.33
  83.0 17.5 %gather_fusion = s32[3328]{0:T(1024)S(1)} fusion(s32[3328]{0:T(1024)S(1)} %subtract_add_fusion, s32[4096]{0:T(1024)S(1)} %pad_clamp_fusion.7), kind=kCustom, calls=%fused_computation.4 | custom fusion | bytes 39936 | tf_op jit(solution)/shard_map/gather | solution.py:18
  100.9 0.8 copy.20
  102.5 26.1 %gather_fusion.2 = s32[4992]{0:T(1024)S(1)} fusion(s32[3328]{0:T(1024)S(1)} %reduce.9, s32[5120]{0:T(1024)S(1)} %pad_clamp_fusion.1), kind=kCustom, calls=%fused_computation.6 | custom fusion | bytes 59904 | tf_op jit(solution)/shard_map/gather | solution.py:27
  130.1 6.5 %gather_fusion.1 = bf16[3328,128]{1,0:T(8,128)(2,1)S(1)} fusion(bf16[4992,128]{1,0:T(8,128)(2,1)S(1)} %bitcast.23, s32[4096]{0:T(1024)S(1)} %pad_clamp_fusion.6), kind=kCustom, calls=%fused_computation.5 | custom fusion | bytes 1717248 | tf_op jit(solution)/shard_map/jit(_take)/gather | solution.py:59
  136.7 0.9 gather.29
  137.8 4.8 convolution_add_fusion
  142.6 2.1 divide_subtract_fusion
  144.7 1.4 broadcast_multiply_fusion
  146.2 6.1 %fusion.12 = f32[128,3456]{1,0:T(8,128)} fusion(bf16[3456,512]{1,0:T(8,128)(2,1)} %all-gather.3.cloned.1.call-done, bf16[3456,512]{1,0:T(8,128)(2,1)} %all-gather.5.cloned.1.call-done, f32[3456]{0:T(1024)S(1)} %copy-done.11, f32[128]{0:T(128)S(1)} %get-tuple-element.14, bf16[128,3328]{1,0:T(8,128)(2,1)S(1)} %broadcast_select_fusion, ...), kind=kOutput, calls=%fused_computation.37 | convolution fusion | flops 909131776 | bytes 9746432 | tf_op jit(solution)/shard_map/dot_general | solution.py:77
  152.2 3.1 fusion.11
  155.4 2.2 reshape.337
  157.6 10.0 %gather_fusion.3 = bf16[4992,128]{1,0:T(8,128)(2,1)S(1)} fusion(bf16[3328,128]{1,0:T(8,128)(2,1)S(1)} %reshape.337, s32[5120]{0:T(1024)S(1)} %copy-done.12), kind=kCustom, calls=%fused_computation.7 | custom fusion | bytes 2575872 | tf_op jit(solution)/shard_map/jit(_take)/gather | solution.py:81
  167.6 3.9 select_select_fusion
  171.5 7.2 %all-to-all-start.1 = ((bf16[16,312,128]{2,1,0:T(8,128)(2,1)}), bf16[16,312,128]{2,1,0:T(8,128)(2,1)S(1)}, u32[]{:S(2)}, u32[]{:S(2)}) async-start(bf16[16,312,128]{2,1,0:T(8,128)(2,1)} %select_select_fusion), calls=%async_computation.1 | async-start | bytes 2555904 | tf_op jit(solution)/shard_map/all_to_all | solution.py:85
  179.7 31.5 %all-to-all-done.1 = bf16[16,312,128]{2,1,0:T(8,128)(2,1)S(1)} async-done(((bf16[16,312,128]{2,1,0:T(8,128)(2,1)}), bf16[16,312,128]{2,1,0:T(8,128)(2,1)S(1)}, u32[]{:S(2)}, u32[]{:S(2)}) %all-to-all-start.1) | async-done | bytes 1277984 | tf_op jit(solution)/shard_map/all_to_all | solution.py:85
  211.2 25.9 %scatter_custom_fusion.1 = f32[1024,128]{1,0:T(8,128)S(1)} fusion(s32[4992]{0:T(1024)S(1)} %fusion.17, bf16[4992,128]{1,0:T(8,128)(2,1)S(1)} %bitcast.24, f32[]{:T(128)} %constant.48.clone.1), kind=kCustom, calls=%fused_computation.20 | custom fusion | flops 1277952 | bytes 1802244 | tf_op jit(solution)/shard_map/scatter-add | solution.py:89
  237.1 28.6 %scatter_custom_fusion.2 = f32[1024,128]{1,0:T(8,128)S(1)} fusion(f32[1024,128]{1,0:T(8,128)S(1)} %scatter_custom_fusion.1, s32[4992]{0:T(1024)S(1)} %fusion.19, bf16[4992,128]{1,0:T(8,128)(2,1)S(1)} %bitcast.25), kind=kCustom, calls=%fused_computation.18 | custom fusion | flops 1277952 | bytes 1802240 | tf_op jit(solution)/shard_map/scatter-add | solution.py:89
  265.7 28.6 %scatter_custom_fusion.3 = f32[1024,128]{1,0:T(8,128)S(1)} fusion(f32[1024,128]{1,0:T(8,128)S(1)} %scatter_custom_fusion.2, s32[4992]{0:T(1024)S(1)} %fusion.20, bf16[4992,128]{1,0:T(8,128)(2,1)S(1)} %bitcast.26), kind=kCustom, calls=%fused_computation.16 | custom fusion | flops 1277952 | bytes 1802240 | tf_op jit(solution)/shard_map/scatter-add | solution.py:89
  294.3 28.6 %scatter_custom_fusion.4 = f32[1024,128]{1,0:T(8,128)S(1)} fusion(f32[1024,128]{1,0:T(8,128)S(1)} %scatter_custom_fusion.3, s32[4992]{0:T(1024)S(1)} %fusion.21, bf16[4992,128]{1,0:T(8,128)(2,1)S(1)} %bitcast.27), kind=kCustom, calls=%fused_computation.14 | custom fusion | flops 1277952 | bytes 1802240 | tf_op jit(solution)/shard_map/scatter-add | solution.py:89
  323.0 0.8 copy-done.1
  323.8 151.5 %all-reduce.2.cloned.1.call-done = f32[1024,128]{1,0:T(8,128)} async-done(((f32[1024,128]{1,0:T(8,128)}), f32[1024,128]{1,0:T(8,128)}) %all-reduce.2.cloned.1.call-update) | async-done | bytes 524304 | tf_op jit(solution)/shard_map/psum | solution.py:90
  475.3 1.2 multiply_reduce_fusion
  477.1 2.0 negate_divide_fusion
  (95 shorter events, 7.7 us)
Async XLA Ops:
  7.2 3.5 copy-start
  7.2 130.6 %all-gather.3.cloned.1.call-start = ((), (), s32[]{:S(2)}) async-start(), calls=%async_computation.2 | async-start | bytes 3760128 | tf_op jit(solution)/shard_map/all_gather | solution.py:62
  7.9 129.9 %all-gather.5.cloned.1.call-start = ((), (), s32[]{:S(2)}) async-start(), calls=%async_computation.3 | async-start | bytes 3760128 | tf_op jit(solution)/shard_map/all_gather | solution.py:63
  10.0 0.6 copy-start.3
  10.0 0.6 copy-start.5
  10.0 0.6 copy-start.7
  10.1 0.6 copy-start.9
  56.3 12.8 %copy-start.14 = (s32[1,1,3328]{2,1,0:T(1,128)S(1)}, s32[1,1,3328]{2,1,0:T(1,128)}, u32[]{:S(2)}) copy-start(s32[1,1,3328]{2,1,0:T(1,128)} %param.17) | copy-start | bytes 39940
  56.3 73.9 %all-to-all-start = ((bf16[16,312,128]{2,1,0:T(8,128)(2,1)}), bf16[16,312,128]{2,1,0:T(8,128)(2,1)S(1)}, u32[]{:S(2)}, u32[]{:S(2)}) async-start(bf16[16,312,128]{2,1,0:T(8,128)(2,1)} %bitcast.28), calls=%async_computation | async-start | bytes 2555904 | tf_op jit(solution)/shard_map/all_to_all | solution.py:54
  83.0 18.8 %copy-start.11 = (f32[3456]{0:T(1024)S(1)}, f32[3456]{0:T(1024)}, u32[]{:S(2)}) copy-start(f32[3456]{0:T(1024)} %param.23) | copy-start | bytes 41476
  136.7 1.2 copy-start.2
  137.7 4.9 %copy-start.13 = (f32[3456,1]{0,1:T(1,128)S(1)}, f32[3456,1]{0,1:T(1,128)}, u32[]{:S(2)}) copy-start(f32[3456,1]{0,1:T(1,128)} %reshape.462) | copy-start | bytes 41476
  137.8 4.9 %copy-start.18 = (s32[128]{0:T(128)S(1)}, s32[128]{0:T(128)}, u32[]{:S(2)}) copy-start(s32[128]{0:T(128)} %param.19) | copy-start | bytes 1540
  152.2 5.3 %copy-start.12 = (s32[5120]{0:T(1024)S(1)}, s32[5120]{0:T(1024)}, u32[]{:S(2)}) copy-start(s32[5120]{0:T(1024)} %pad_clamp_fusion) | copy-start | bytes 61444
  157.5 10.0 %copy-start.15 = (pred[16,312]{1,0:T(8,128)(4,1)S(1)}, pred[16,312]{1,0:T(8,128)(4,1)}, u32[]{:S(2)}) copy-start(pred[16,312]{1,0:T(8,128)(4,1)} %get-tuple-element.20) | copy-start | bytes 14980
  157.6 10.0 %copy-start.16 = (pred[16,312]{1,0:T(8,128)(4,1)S(1)}, pred[16,312]{1,0:T(8,128)(4,1)}, u32[]{:S(2)}) copy-start(pred[16,312]{1,0:T(8,128)(4,1)} %get-tuple-element.21) | copy-start | bytes 14980
  167.6 11.4 %copy-start.10 = (s32[16,312]{1,0:T(8,128)S(1)}, s32[16,312]{1,0:T(8,128)}, u32[]{:S(2)}) copy-start(s32[16,312]{1,0:T(8,128)} %copy-done.9) | copy-start | bytes 59908
  167.6 11.5 %copy-start.8 = (s32[16,312]{1,0:T(8,128)S(1)}, s32[16,312]{1,0:T(8,128)}, u32[]{:S(2)}) copy-start(s32[16,312]{1,0:T(8,128)} %copy-done.7) | copy-start | bytes 59908
  167.6 11.6 %copy-start.6 = (s32[16,312]{1,0:T(8,128)S(1)}, s32[16,312]{1,0:T(8,128)}, u32[]{:S(2)}) copy-start(s32[16,312]{1,0:T(8,128)} %copy-done.5) | copy-start | bytes 59908
  167.6 11.7 %copy-start.4 = (s32[16,312]{1,0:T(8,128)S(1)}, s32[16,312]{1,0:T(8,128)}, u32[]{:S(2)}) copy-start(s32[16,312]{1,0:T(8,128)} %copy-done.3) | copy-start | bytes 59908
  171.5 39.8 %all-to-all-start.1 = ((bf16[16,312,128]{2,1,0:T(8,128)(2,1)}), bf16[16,312,128]{2,1,0:T(8,128)(2,1)S(1)}, u32[]{:S(2)}, u32[]{:S(2)}) async-start(bf16[16,312,128]{2,1,0:T(8,128)(2,1)} %select_select_fusion), calls=%async_computation.1 | async-start | bytes 2555904 | tf_op jit(solution)/shard_map/all_to_all | solution.py:85
  178.7 296.6 %all-reduce.2.cloned.1.call-start = ((), (), s32[]{:S(2)}) async-start(), calls=%async_computation.4 | async-start | bytes 1048576 | tf_op jit(solution)/shard_map/psum | solution.py:90
  265.7 210.8 %copy-start.17 = (f32[1024]{0:T(1024)S(1)}, f32[1024]{0:T(1024)}, u32[]{:S(2)}) copy-start(f32[1024]{0:T(1024)} %param.14) | copy-start | bytes 12292
  323.0 0.8 copy-start.1
Sparse Core Ops, SparseCore 0:
  10.1 50.6 all-gather.2
  63.0 59.1 all-gather.4
  323.9 151.3 all-reduce.1
where the time goes:
time: 489 us; the launch traced here: 486 us
  waiting for transfers between devices  184 us (38%)
  other arithmetic  134 us (27%)
  local copies, waits for them, and re-layouts  121 us (25%)
  starting transfers between devices  19.4 us (4%)
  between operations  14.4 us (3%)
  matrix products  12.9 us (3%)
    psum x1, waiting for transfers between devices, local(): summed = lax.psum(local_grads, 'replica')  151 us
    scatter-add x4, other arithmetic, local(): local_grads.at[row_ids[:, member].reshape(-1)].add(returned_rows)  112 us
    all_to_all x1, waiting for transfers between devices, local(): lax.all_to_all(outgoing, 'table', split_axis=0, concat_axis=0, tiled=True)  31.5 us
    gather x3, local copies, waits for them, and re-layouts, local(): jnp.take(emb_table, row_ids[:, member].reshape(-1), axis=0)  28.4 us
    gather x2, local copies, waits for them, and re-layouts, slot_bags(): return (permute[position], is_live)  26.2 us
    gather x2, local copies, waits for them, and re-layouts, bag_sources(): return flat_slot[inverse]  17.7 us
    scatter x1, local copies, waits for them, and re-layouts, bag_sources(): inverse = jnp.zeros((bag_count,), jnp.int32).at[permute].set(counter)  12.9 us
    all_to_all x1, starting transfers between devices, local(): lax.all_to_all(slot_pool, 'table', split_axis=0, concat_axis=0, tiled=True)  11.8 us
  transfers between devices with their start and end apart: 5, of which 2 were waited for; matrix products, arithmetic and copies ran while one was open for 24% of the time, Pallas kernels for 0%

commit v1 on v0

v1 whole, which is shorter than its diff:
```python
import jax
import jax.numpy as jnp
from jax import lax
from jax.experimental import pallas as pl
from jax.experimental.pallas import tpu as pltpu
from jax.sharding import PartitionSpec as P

EPSILON = 1e-08
MESH = pl.DeviceIdType.MESH
CHUNK = 384
BLOCK = 256


def multi_hot(ids, rows, store):
    hot, n = ids.shape
    row = lax.broadcasted_iota(jnp.int32, (BLOCK, n), 0).astype(jnp.float32).astype(jnp.bfloat16)
    one = jnp.ones((BLOCK, n), jnp.bfloat16)
    zero = jnp.zeros((BLOCK, n), jnp.bfloat16)
    for first in range(0, rows, BLOCK):
        near = jnp.clip(ids - first, -1, BLOCK).astype(jnp.float32).astype(jnp.bfloat16)
        total = None
        for member in range(hot):
            hit = jnp.where(row == near[member : member + 1, :], one, zero)
            total = hit if total is None else total + hit
        store(first, total)


def pool_kernel(ids_ref, table_ref, out_ref, table_t, hits):
    rows = table_ref.shape[0]
    width = table_ref.shape[1]

    @pl.when(pl.program_id(0) == 0)
    def _():
        turned = table_ref[...].T
        high = turned.astype(jnp.bfloat16)
        table_t[:width, :] = high
        table_t[width:, :] = (turned - high.astype(jnp.float32)).astype(jnp.bfloat16)

    def store(first, block):
        hits[first : first + BLOCK, :] = block

    multi_hot(ids_ref[...], rows, store)
    both = jnp.dot(table_t[...], hits[...], preferred_element_type=jnp.float32)
    out_ref[...] = (both[:width, :] + both[width:, :]).T.astype(jnp.bfloat16)


def pool(ids, table):
    hot, slots = ids.shape
    rows, width = table.shape
    return pl.pallas_call(
        pool_kernel,
        grid=(slots // CHUNK,),
        in_specs=[
            pl.BlockSpec((hot, CHUNK), lambda i: (0, i)),
            pl.BlockSpec((rows, width), lambda i: (0, 0)),
        ],
        out_specs=pl.BlockSpec((CHUNK, width), lambda i: (i, 0)),
        out_shape=jax.ShapeDtypeStruct((slots, width), jnp.bfloat16),
        scratch_shapes=[
            pltpu.VMEM((2 * width, rows), jnp.bfloat16),
            pltpu.VMEM((rows, CHUNK), jnp.bfloat16),
        ],
        name="pool",
    )(ids, table)


def finish_kernel(
    ids_ref, outgoing_ref, accum_ref, update_ref, squares_ref,
    arrived, hits, grads, parts, result,
    back_send, back_recv, part_send, part_recv, result_send, result_recv, own_sem,
):
    shards, capacity, width = outgoing_ref.shape
    padded = arrived.shape[1]
    copies, share, _ = grads.shape
    rows = copies * share
    own_table = lax.axis_index("table")
    own_copy = lax.axis_index("replica")

    barrier = pltpu.get_barrier_semaphore()

    def greet_table(d, carry):
        pl.semaphore_signal(barrier, inc=1, device_id=(own_copy, lax.rem(own_table + d, shards)), device_id_type=MESH)
        return carry

    def greet_copy(d, carry):
        pl.semaphore_signal(barrier, inc=1, device_id=(lax.rem(own_copy + d, copies), own_table), device_id_type=MESH)
        return carry

    lax.fori_loop(1, shards, greet_table, 0)
    lax.fori_loop(1, copies, greet_copy, 0)
    pl.semaphore_wait(barrier, shards + copies - 2)

    def back(d):
        peer = lax.rem(own_table + d, shards)
        return pltpu.make_async_remote_copy(
            src_ref=outgoing_ref.at[peer],
            dst_ref=arrived.at[own_table, pl.ds(0, capacity)],
            send_sem=back_send.at[d],
            recv_sem=back_recv.at[d],
            device_id=(own_copy, peer),
            device_id_type=MESH,
        )

    def start_back(d, carry):
        back(d).start()
        return carry

    lax.fori_loop(1, shards, start_back, 0)
    own = pltpu.make_async_copy(outgoing_ref.at[own_table], arrived.at[own_table, pl.ds(0, capacity)], own_sem)
    own.start()

    def prepare(s, carry):
        arrived[s, pl.ds(capacity, padded - capacity), :] = jnp.zeros((padded - capacity, width), jnp.bfloat16)

        def store(first, block):
            hits[s, first : first + BLOCK, :] = block

        multi_hot(ids_ref[s], rows, store)
        return carry

    lax.fori_loop(0, shards, prepare, 0)
    own.wait()
    grads[...] = jnp.dot(hits[own_table], arrived[own_table], preferred_element_type=jnp.float32).reshape(grads.shape)

    def add(d, carry):
        source = lax.rem(own_table + shards - d, shards)
        back(d).wait_recv()
        term = jnp.dot(hits[source], arrived[source], preferred_element_type=jnp.float32)
        grads[...] += term.reshape(grads.shape)
        return carry

    lax.fori_loop(1, shards, add, 0)

    def part(d):
        peer = lax.rem(own_copy + d, copies)
        return pltpu.make_async_remote_copy(
            src_ref=grads.at[peer],
            dst_ref=parts.at[d],
            send_sem=part_send.at[d],
            recv_sem=part_recv.at[d],
            device_id=(peer, own_table),
            device_id_type=MESH,
        )

    def start_part(d, carry):
        part(d).start()
        return carry

    lax.fori_loop(1, copies, start_part, 0)

    def add_part(d, total):
        part(d).wait_recv()
        return total + parts[d]

    total = lax.fori_loop(1, copies, add_part, grads[own_copy])
    diagonal = lax.broadcasted_iota(jnp.int32, (share, width), 0) == lax.broadcasted_iota(jnp.int32, (share, width), 1)
    before = jnp.sum(jnp.where(diagonal, accum_ref[pl.ds(own_copy, 1), :], 0.0), axis=1, keepdims=True)
    accum = before + jnp.sum(total * total, axis=1, keepdims=True) * (1.0 / width)
    result[own_copy, :share, :] = -total / (jnp.sqrt(accum) + EPSILON)
    squares = jnp.sum(jnp.where(diagonal, accum, 0.0), axis=0, keepdims=True)
    result[own_copy, pl.ds(share, 8), :] = jnp.broadcast_to(squares, (8, width))

    def share_out(d):
        peer = lax.rem(own_copy + d, copies)
        return pltpu.make_async_remote_copy(
            src_ref=result.at[own_copy],
            dst_ref=result.at[own_copy],
            send_sem=result_send.at[d],
            recv_sem=result_recv.at[d],
            device_id=(peer, own_table),
            device_id_type=MESH,
        )

    def start_share(d, carry):
        share_out(d).start()
        return carry

    lax.fori_loop(1, copies, start_share, 0)

    def write(source):
        update_ref[source] = result[source, :share, :]
        squares_ref[pl.ds(source, 1), :] = result[source, pl.ds(share, 1), :]

    write(own_copy)

    def take(d, carry):
        share_out(d).wait_recv()
        write(lax.rem(own_copy + copies - d, copies))
        return carry

    lax.fori_loop(1, copies, take, 0)

    def sent_back(d, carry):
        back(d).wait_send()
        return carry

    def sent_copy(d, carry):
        part(d).wait_send()
        share_out(d).wait_send()
        return carry

    lax.fori_loop(1, shards, sent_back, 0)
    lax.fori_loop(1, copies, sent_copy, 0)


def finish(ids, outgoing, accum, rows, copies):
    shards, hot, padded = ids.shape
    width = outgoing.shape[2]
    capacity = outgoing.shape[1]
    share = rows // copies
    vmem = pl.BlockSpec(memory_space=pltpu.VMEM)
    return pl.pallas_call(
        finish_kernel,
        in_specs=[vmem] * 3,
        out_specs=[vmem] * 2,
        out_shape=[
            jax.ShapeDtypeStruct((copies, share, width), jnp.float32),
            jax.ShapeDtypeStruct((copies, width), jnp.float32),
        ],
        scratch_shapes=[
            pltpu.VMEM((shards, padded, width), jnp.bfloat16),
            pltpu.VMEM((shards, rows, padded), jnp.bfloat16),
            pltpu.VMEM((copies, share, width), jnp.float32),
            pltpu.VMEM((copies, share, width), jnp.float32),
            pltpu.VMEM((copies, share + 8, width), jnp.float32),
            pltpu.SemaphoreType.DMA((shards,)),
            pltpu.SemaphoreType.DMA((shards,)),
            pltpu.SemaphoreType.DMA((copies,)),
            pltpu.SemaphoreType.DMA((copies,)),
            pltpu.SemaphoreType.DMA((copies,)),
            pltpu.SemaphoreType.DMA((copies,)),
            pltpu.SemaphoreType.DMA,
        ],
        compiler_params=pltpu.CompilerParams(collective_id=1, has_side_effects=True),
        name="finish",
    )(ids, outgoing, accum)


def cross_kernel(
    place_ref, live_ref, start_ref, arrived_ref, dense_ref, labels_ref, in_hbm, out_hbm, bias_ref, head_ref,
    logits_ref, outgoing_ref,
    slots, bags, inputs, mixed, scaled, w_in, w_out, sems,
):
    shards, capacity, width = arrived_ref.shape
    batch = dense_ref.shape[0]
    features = inputs.shape[1] // width - 1
    load_in = pltpu.make_async_copy(in_hbm, w_in, sems.at[0])
    load_out = pltpu.make_async_copy(out_hbm, w_out, sems.at[1])
    load_in.start()
    load_out.start()

    def widen(s, carry):
        first = pl.multiple_of(s * capacity, 8)
        slots[pl.ds(first, capacity), :] = arrived_ref[s].astype(jnp.float32)
        return carry

    lax.fori_loop(0, shards, widen, 0)

    def arrange(s, carry):
        base = start_ref[s]

        def eight(i, inner):
            row = pl.multiple_of(s * capacity + i * 8, 8)
            for j in range(8):
                bags[pl.ds(place_ref[base + i * 8 + j], 1), :] = slots[pl.ds(row + j, 1), :]
            return inner

        lax.fori_loop(0, (live_ref[s] + 7) // 8, eight, 0)
        return carry

    lax.fori_loop(0, shards, arrange, 0)

    inputs[:, :width] = dense_ref[...]
    for f in range(features):
        inputs[:, (f + 1) * width : (f + 2) * width] = bags[f * batch : (f + 1) * batch, :].astype(jnp.bfloat16)

    rank = w_in.shape[1]
    columns = inputs.shape[1]
    step = 3 * width
    contract = (((1,), (1,)), ((), ()))
    load_in.wait()
    hidden = jnp.dot(inputs[...], w_in[...], preferred_element_type=jnp.float32).astype(jnp.bfloat16)
    load_out.wait()
    total = jnp.zeros((batch, 1), jnp.float32)
    for first in range(0, columns, step):
        part = slice(first, first + step)
        x = inputs[:, part].astype(jnp.float32)
        m = lax.dot_general(hidden, w_out[part, :], contract, preferred_element_type=jnp.float32) + bias_ref[:, part]
        mixed[:, part] = m
        total = total + jnp.sum((x * m + x) * head_ref[:, part], axis=1, keepdims=True)
    diagonal = lax.broadcasted_iota(jnp.int32, (batch, batch), 0) == lax.broadcasted_iota(jnp.int32, (batch, batch), 1)
    logits_ref[...] = jnp.sum(jnp.where(diagonal, total, 0.0), axis=0, keepdims=True)
    marks = jnp.sum(jnp.where(diagonal, labels_ref[...].astype(jnp.float32), 0.0), axis=1, keepdims=True)
    slope = 1.0 / (1.0 + jnp.exp(-total)) - marks
    for first in range(0, columns, step):
        part = slice(first, first + step)
        x = inputs[:, part].astype(jnp.float32)
        scaled[:, part] = (slope * head_ref[:, part] * x).astype(jnp.bfloat16)
    hidden_grad = jnp.dot(scaled[...], w_out[...], preferred_element_type=jnp.float32).astype(jnp.bfloat16)
    for first in range(width, columns, 2 * width):
        part = slice(first, first + 2 * width)
        back = lax.dot_general(hidden_grad, w_in[part, :], contract, preferred_element_type=jnp.float32)
        grad = slope * head_ref[:, part] * (mixed[:, part] + 1.0) + back
        row = (first // width - 1) * batch
        bags[row : row + batch, :] = grad[:, :width]
        bags[row + batch : row + 2 * batch, :] = grad[:, width:]

    def collect(s, carry):
        base = start_ref[s]

        def eight(i, inner):
            row = pl.multiple_of(s * capacity + i * 8, 8)
            for j in range(8):
                slots[pl.ds(row + j, 1), :] = bags[pl.ds(place_ref[base + i * 8 + j], 1), :]
            return inner

        lax.fori_loop(0, (live_ref[s] + 7) // 8, eight, 0)
        return carry

    lax.fori_loop(0, shards, collect, 0)
    which = lax.broadcasted_iota(jnp.int32, (capacity, width), 0)

    def narrow(s, carry):
        first = pl.multiple_of(s * capacity, 8)
        value = slots[pl.ds(first, capacity), :]
        outgoing_ref[s] = jnp.where(which < live_ref[s], value, 0.0).astype(jnp.bfloat16)
        return carry

    lax.fori_loop(0, shards, narrow, 0)


def cross(place, live, start, arrived, dense, labels, full_in, full_out, bias, head):
    shards, capacity, width = arrived.shape
    batch = dense.shape[0]
    columns, rank = full_in.shape
    features = columns // width - 1
    vmem = pl.BlockSpec(memory_space=pltpu.VMEM)
    smem = pl.BlockSpec(memory_space=pltpu.SMEM)
    hbm = pl.BlockSpec(memory_space=pl.ANY)
    return pl.pallas_call(
        cross_kernel,
        in_specs=[smem, smem, smem, vmem, vmem, vmem, hbm, hbm, vmem, vmem],
        out_specs=[vmem, vmem],
        out_shape=[
            jax.ShapeDtypeStruct((1, batch), jnp.float32),
            jax.ShapeDtypeStruct((shards, capacity, width), jnp.bfloat16),
        ],
        scratch_shapes=[
            pltpu.VMEM((shards * capacity, width), jnp.float32),
            pltpu.VMEM((features * batch + 8, width), jnp.float32),
            pltpu.VMEM((batch, columns), jnp.bfloat16),
            pltpu.VMEM((batch, columns), jnp.float32),
            pltpu.VMEM((batch, columns), jnp.bfloat16),
            pltpu.VMEM((columns, rank), jnp.bfloat16),
            pltpu.VMEM((columns, rank), jnp.bfloat16),
            pltpu.SemaphoreType.DMA((2,)),
        ],
        name="cross",
    )(place, live, start, arrived, dense, labels, full_in, full_out, bias, head)


def local(
    emb_table,
    row_accum,
    look_rows,
    live_counts,
    bag_order,
    dense_emb,
    labels,
    cross_in,
    cross_out,
    cross_bias,
    head_weight,
):
    shards = lax.axis_size("table")
    copies = lax.axis_size("replica")
    own_index = lax.axis_index("table")
    rows, width = emb_table.shape
    hot, capacity = look_rows.shape[3:]
    batch = dense_emb.shape[0]
    features = cross_in.shape[0] * shards // width - 1
    ids = look_rows[0, 0].transpose(1, 0, 2).reshape(hot, shards * capacity)
    pooled = pool(ids, emb_table).reshape(shards, capacity, width)
    arrived = lax.all_to_all(pooled, "table", split_axis=0, concat_axis=0, tiled=True)
    live = lax.dynamic_index_in_dim(live_counts[0], own_index, 0, keepdims=False)
    start = jnp.cumsum(live) - live
    order = bag_order[0, 0]
    place = order % features * batch + order // features
    place = jnp.pad(place, (0, 8), constant_values=features * batch)
    full_in = lax.all_gather(cross_in, "table", axis=0, tiled=True)
    full_out = lax.all_gather(cross_out, "table", axis=0, tiled=True)
    logits, outgoing = cross(
        place, live, start, arrived, dense_emb, labels.reshape(1, -1), full_in, full_out,
        cross_bias.reshape(1, -1), head_weight.reshape(1, -1),
    )
    padded = -(-capacity // 128) * 128
    lanes = jnp.pad(look_rows[0, 0], ((0, 0), (0, 0), (0, padded - capacity)), constant_values=-1)
    accum = jnp.pad(row_accum.reshape(copies, rows // copies), ((0, 0), (0, width - rows // copies)))
    update, squares = finish(lanes, outgoing, accum, rows, copies)
    row_update = update.reshape(rows, width)
    new_accum = squares[:, : rows // copies].reshape(rows)
    return (logits.reshape(-1), row_update, new_accum)


def solution(mesh):
    placed = (
        P("table", None),
        P("table"),
        P("replica", "table", None, None, None),
        P("replica", None, None),
        P("replica", "table", None),
        P(("replica", "table"), None),
        P(("replica", "table")),
        P("table", None),
        P("table", None),
        P(),
        P(),
    )
    return jax.shard_map(
        local,
        mesh=mesh,
        in_specs=placed,
        out_specs=(P(("replica", "table")), P("table", None), P("table")),
        check_vma=False,
    )
```

time: 489 us -> 229 us (0.47)
  other arithmetic: 134 us -> 1.62 us
  local copies, waits for them, and re-layouts: 121 us -> 8.87 us
  Pallas kernels: 0 us -> 102 us
  waiting for transfers between devices: 184 us -> 89.2 us
  matrix products: 12.9 us -> 0 us
  starting transfers between devices: 19.4 us -> 12.1 us
    psum x1 -> x0, waiting for transfers between devices: 151 us -> none  [local(): summed = lax.psum(local_grads, 'replica')]
    scatter-add x4 -> x0, other arithmetic: 112 us -> none  [local(): local_grads.at[row_ids[:, member].reshape(-1)].add(returned_rows)]
    pallas_call x0 -> x3, Pallas kernels: none -> 102 us  [the longest x1 73.7 us: finish(): pl.pallas_call(finish_kernel, in_specs=[vmem] * 3, out_specs=[vmem] * 2,...]
    gather x11 -> x0, local copies, waits for them, and re-layouts: 99.9 us -> none  [the longest x3 28.4 us: local(): jnp.take(emb_table, row_ids[:, member].reshape(-1), axis=0)]
    all_gather x2, waiting for transfers between devices: 0.04 us -> 51.4 us  [the longest x1 46.1 us: local(): full_out = lax.all_gather(cross_out, 'table', axis=0, tiled=True)]
    dot_general x3 -> x0, matrix products: 12.9 us -> none  [the longest x1 6.06 us: local(): lax.dot_general(hidden_grad, full_in, contract, preferred_element_type=jn...]
    scatter x1 -> x0, local copies, waits for them, and re-layouts: 12.9 us -> none  [bag_sources(): inverse = jnp.zeros((bag_count,), jnp.int32).at[permute].set(counter)]
    all_to_all x2 -> x1, starting transfers between devices: 19 us -> 12 us  [local(): lax.all_to_all(pooled, 'table', split_axis=0, concat_axis=0, tiled=True)]
  transfers between devices with their start and end apart: 5 -> 3, of which waited for: 2 -> 3; matrix products, arithmetic and copies ran while one was open for 24% -> 3% of each run, Pallas kernels for 0% -> 5%
where the time goes in v1:
time: 229 us; the launch traced here: 228 us
  Pallas kernels  102 us (45%)
  waiting for transfers between devices  89.2 us (39%)
  between operations  14.1 us (6%)
  starting transfers between devices  12.1 us (5%)
  local copies, waits for them, and re-layouts  8.87 us (4%)
    pallas_call x1, Pallas kernels, finish(): pl.pallas_call(finish_kernel, in_specs=[vmem] * 3, out_specs=[vmem] * 2,...  73.7 us
    all_gather x1, waiting for transfers between devices, local(): full_out = lax.all_gather(cross_out, 'table', axis=0, tiled=True)  46.1 us
    all_to_all x1, waiting for transfers between devices, local(): lax.all_to_all(pooled, 'table', split_axis=0, concat_axis=0, tiled=True)  36.4 us
    pallas_call x1, Pallas kernels, cross(): pl.pallas_call(cross_kernel, in_specs=[smem, smem, smem, vmem, vmem, vmem...  16.7 us
    all_to_all x1, starting transfers between devices, local(): lax.all_to_all(pooled, 'table', split_axis=0, concat_axis=0, tiled=True)  12 us
    pallas_call x1, Pallas kernels, pool(): pl.pallas_call(pool_kernel, grid=(slots // CHUNK,), in_specs=[pl.BlockSpe...  11.9 us
    all_gather x1, waiting for transfers between devices, local(): full_in = lax.all_gather(cross_in, 'table', axis=0, tiled=True)  5.31 us
  transfers between devices with their start and end apart: 3, of which 3 were waited for; matrix products, arithmetic and copies ran while one was open for 3% of the time, Pallas kernels for 5%

profile of v1, /device:TPU:1, one launch (start us, length us, event | category | flops | bytes accessed | tf_op | source)
XLA Modules:
  0.0 228.1 jit_solution(17205834285116104)
XLA Ops:
  7.2 0.0 all-gather.3.cloned.1.call-start
  7.2 0.7 all-gather.3.cloned.1.call-update
  7.9 0.0 all-gather.5.cloned.1.call-start
  7.9 0.7 all-gather.5.cloned.1.call-update
  8.6 0.9 copy.16
  9.5 0.8 reshape.71.ids_ref
  10.3 11.9 %pool.1 = bf16[4992,128]{1,0:T(8,128)(2,1)} custom-call(s32[4,4992]{1,0:T(4,128)} %reshape.71.ids_ref, f32[1024,128]{1,0:T(8,128)} %table_ref.1), custom_call_target="tpu_custom_call" | custom-call | tf_op jit(solution)/shard_map/pool/pallas_call | solution.py:50
  22.2 0.0 copy-start.2
  22.2 0.0 copy-start.1
  22.2 12.0 %all-to-all-start = ((bf16[16,312,128]{2,1,0:T(8,128)(2,1)}), bf16[16,312,128]{2,1,0:T(8,128)(2,1)S(1)}, u32[]{:S(2)}, u32[]{:S(2)}) async-start(bf16[16,312,128]{2,1,0:T(8,128)(2,1)} %bitcast.13), calls=%async_computation | async-start | bytes 2555904 | tf_op jit(solution)/shard_map/all_to_all | solution.py:384
  34.2 0.7 fusion.2
  34.9 0.1 copy.15
  35.0 0.1 reduce.3
  35.1 0.0 copy-done.3
  35.1 0.6 reshape.74.bias_ref
  35.7 0.0 copy-done.4
  35.7 0.6 reshape.75.head_ref
  36.3 0.1 reshape.77
  36.4 0.1 compare_reduce_fusion
  36.5 0.1 divide_reduce_fusion
  36.6 0.6 pad.12.place_ref
  37.2 0.0 copy-done.1
  37.2 0.7 pad.13.ids_ref
  37.9 0.6 pad.14.accum_ref
  38.5 1.3 fusion.4
  39.8 36.4 %all-to-all-done.arrived_ref = bf16[16,312,128]{2,1,0:T(8,128)(2,1)S(1)} async-done(((bf16[16,312,128]{2,1,0:T(8,128)(2,1)}), bf16[16,312,128]{2,1,0:T(8,128)(2,1)S(1)}, u32[]{:S(2)}, u32[]{:S(2)}) %all-to-all-start) | async-done | bytes 1277984 | tf_op jit(solution)/shard_map/all_to_all | solution.py:384
  76.2 5.3 %all-gather.3.cloned.1.call-done.in_hbm = bf16[3456,512]{1,0:T(8,128)(2,1)} async-done(((bf16[216,512]{1,0:T(8,128)(2,1)}), bf16[3456,512]{1,0:T(8,128)(2,1)}) %all-gather.3.cloned.1.call-update) | async-done | bytes 3538960 | tf_op jit(solution)/shard_map/all_gather | solution.py:390
  81.5 46.1 %all-gather.5.cloned.1.call-done.out_hbm = bf16[3456,512]{1,0:T(8,128)(2,1)} async-done(((bf16[216,512]{1,0:T(8,128)(2,1)}), bf16[3456,512]{1,0:T(8,128)(2,1)}) %all-gather.5.cloned.1.call-update) | async-done | bytes 3538960 | tf_op jit(solution)/shard_map/all_gather | solution.py:391
  127.6 16.7 %cross.1 = (f32[1,128]{1,0:T(1,128)}, bf16[16,312,128]{2,1,0:T(8,128)(2,1)}) custom-call(s32[3336]{0:T(1024)} %pad.12.place_ref, s32[16]{0:T(128)} %get-tuple-element.14.live_ref, s32[16]{0:T(128)} %get-tuple-element.13.start_ref, bf16[16,312,128]{2,1,0:T(8,128)(2,1)} %copy-done, bf16[128,128]{1,0:T(8,128)(2,1)} %dense_ref.1, s32[1,128]{1,0:T(1,128)} %bitcast.18, ...), custom_call_target="tpu_custom_call" | custom-call | tf_op jit(solution)/shard_map/cross/pallas_call | solution.py:340
  144.3 73.7 %finish.1 = (f32[32,32,128]{2,1,0:T(8,128)}, f32[32,128]{1,0:T(8,128)}) custom-call(s32[16,4,384]{2,1,0:T(4,128)} %pad.13.ids_ref, bf16[16,312,128]{2,1,0:T(8,128)(2,1)} %get-tuple-element.8.outgoing_ref, f32[32,128]{1,0:T(8,128)} %pad.14.accum_ref), custom_call_target="tpu_custom_call" | custom-call | tf_op jit(solution)/shard_map/finish/pallas_call | solution.py:212
  218.0 1.4 reshape.79
  219.4 1.9 copy.18
  (9 shorter events, 0.1 us)
Async XLA Ops:
  7.2 74.3 %all-gather.3.cloned.1.call-start = ((), (), s32[]{:S(2)}) async-start(), calls=%async_computation.1 | async-start | bytes 3760128 | tf_op jit(solution)/shard_map/all_gather | solution.py:390
  7.9 119.7 %all-gather.5.cloned.1.call-start = ((), (), s32[]{:S(2)}) async-start(), calls=%async_computation.2 | async-start | bytes 3760128 | tf_op jit(solution)/shard_map/all_gather | solution.py:391
  22.2 12.9 %copy-start.3 = (f32[3456]{0:T(1024)S(1)}, f32[3456]{0:T(1024)}, u32[]{:S(2)}) copy-start(f32[3456]{0:T(1024)} %param.20) | copy-start | bytes 41476
  22.2 13.6 %copy-start.4 = (f32[3456]{0:T(1024)S(1)}, f32[3456]{0:T(1024)}, u32[]{:S(2)}) copy-start(f32[3456]{0:T(1024)} %param.21) | copy-start | bytes 41476
  22.2 14.2 %copy-start.5 = (f32[1024]{0:T(1024)S(1)}, f32[1024]{0:T(1024)}, u32[]{:S(2)}) copy-start(f32[1024]{0:T(1024)} %param.12) | copy-start | bytes 12292
  22.2 14.2 %copy-start.2 = (s32[1,1,3328]{2,1,0:T(1,128)S(1)}, s32[1,1,3328]{2,1,0:T(1,128)}, u32[]{:S(2)}) copy-start(s32[1,1,3328]{2,1,0:T(1,128)} %param.15) | copy-start | bytes 39940
  22.2 15.0 %copy-start.1 = (s32[1,1,16,4,312]{4,3,2,1,0:T(4,128)S(1)}, s32[1,1,16,4,312]{4,3,2,1,0:T(4,128)}, u32[]{:S(2)}) copy-start(s32[1,1,16,4,312]{4,3,2,1,0:T(4,128)} %param.13) | copy-start | bytes 239620
  22.2 54.0 %all-to-all-start = ((bf16[16,312,128]{2,1,0:T(8,128)(2,1)}), bf16[16,312,128]{2,1,0:T(8,128)(2,1)S(1)}, u32[]{:S(2)}, u32[]{:S(2)}) async-start(bf16[16,312,128]{2,1,0:T(8,128)(2,1)} %bitcast.13), calls=%async_computation | async-start | bytes 2555904 | tf_op jit(solution)/shard_map/all_to_all | solution.py:384
  76.2 51.4 %copy-start = (bf16[16,312,128]{2,1,0:T(8,128)(2,1)}, bf16[16,312,128]{2,1,0:T(8,128)(2,1)S(1)}, u32[]{:S(2)}) copy-start(bf16[16,312,128]{2,1,0:T(8,128)(2,1)S(1)} %all-to-all-done.arrived_ref) | copy-start | bytes 3833860
Sparse Core Ops, SparseCore 0:
  10.1 71.3 all-gather.2
  83.6 43.8 all-gather.4
